TPU v7x, 256 devices: a whole 4x4x8 slice. The times are simulated.
256 devices in a mesh: group: 4 (over x), leaf: 64 (over z, y, core).
Axes of the slice: x: 4, y: 4, z: 8, core: 2. Of those that a mesh axis runs over, the one named last changes fastest.
Arguments:
- right_sides: float32 [16, 1048576], P(None, ('group', 'leaf')), may hold values from -6 to 6
- near_blocks: float32 [16384, 8, 4096], P(('group', 'leaf')), may hold values from -0.375 to 0.375
- near_source: int32 [16384, 8], P(('group', 'leaf')), may hold values from 0 to 16383, as said below
- near_count: int32 [16384], P(('group', 'leaf')), may hold values from 1 to 8
- basis: float32 [16384, 2048], P(('group', 'leaf')), may hold values from -0.75 to 0.75
- leaf_source: int32 [16384, 8], P(('group', 'leaf')), may hold values from 0 to 16383
- leaf_coupling: float32 [16384, 8, 1024], P(('group', 'leaf')), may hold values from -0.375 to 0.375
- leaf_transfer: float32 [16384, 1024], P(('group', 'leaf')), may hold values from -1 to 1
- cluster_source: int32 [1024, 8], P(('group', 'leaf')), may hold values from 0 to 255
- cluster_coupling: float32 [1024, 8, 1024], P(('group', 'leaf')), may hold values from -0.09375 to 0.09375
- cluster_transfer: float32 [1024, 1024], P(('group', 'leaf')), may hold values from -1 to 1
- group_coupling: float32 [4, 4, 1024], P('group'), may hold values from -0.0078125 to 0.0078125
Outputs:
- applied: float32 [16, 1048576], P(None, ('group', 'leaf'))
Inputs may be any that keep to these rules, and one draw needn't show every extreme that they name: near_source[t, j] and leaf_source[t, j] name a leaf held by the same device as t or by the device just before or after it in the order of devices.
All inputs are finite; a program needn't handle non-finite values.
Results may differ from a plain program's by a relative error of at most 0.0001.
Values sent between devices are 32-bit elements; how exact they have to be, the bound alone decides.
No kernel may reach another device: no remote copies, remote signals or barrier semaphores. Data moves between devices by JAX's collectives and lax.ppermute only.
A program may use at most 128 MiB of HBM per device.

v0:
```python
import jax
import jax.numpy as jnp
from jax import lax
from jax.sharding import PartitionSpec as P

LEAF = 64
K = 32
RHS = 16
FAR0 = 8
FAR1 = 8
highest_precision = lax.Precision.HIGHEST


def extended(value, sides, width):
    for axis, dim in sides:
        size, length = (lax.axis_size(axis), value.shape[dim])
        up = [(i, (i + 1) % size) for i in range(size - 1)]
        down = [(j, i) for i, j in up]
        last = lax.slice_in_dim(value, length - width, length, axis=dim)
        leading = lax.slice_in_dim(value, 0, width, axis=dim)
        before = lax.ppermute(last, axis, up)
        after = lax.ppermute(leading, axis, down)
        value = jnp.concatenate([before, value, after], axis=dim)
    return value


def per_device(
    right_sides,
    near_blocks,
    near_source,
    near_count,
    basis,
    leaf_source,
    leaf_coupling,
    leaf_transfer,
    cluster_source,
    cluster_coupling,
    cluster_transfer,
    group_coupling,
):
    leaves_here = near_blocks.shape[0]
    clusters_here = cluster_coupling.shape[0]
    ngroups = lax.axis_size("group")
    device = lax.axis_index(("group", "leaf"))
    blocks = right_sides.reshape(RHS, leaves_here, LEAF).transpose(1, 0, 2)
    bases = basis.reshape(leaves_here, K, LEAF)
    leaf_coef = jnp.einsum("tka,tra->tkr", bases, blocks, precision=highest_precision)
    coef_rows = leaf_coef.transpose(2, 0, 1).reshape(RHS, leaves_here * K)
    point_ext = extended(right_sides, ((("group", "leaf"), 1),), leaves_here * LEAF)
    coef_ext = extended(coef_rows, ((("group", "leaf"), 1),), leaves_here * K)
    window_start = (device - 1) * leaves_here
    near_local = near_source - window_start
    point_blocks = point_ext.reshape(RHS, 3 * leaves_here, LEAF).transpose(1, 0, 2)
    busiest = jnp.max(near_count)

    def near_step(slot_index, running):
        picked = jnp.take(point_blocks, near_local[:, slot_index], axis=0)
        slab = lax.dynamic_index_in_dim(near_blocks, slot_index, axis=1, keepdims=False).reshape(
            leaves_here, LEAF, LEAF
        )
        live = (near_count > slot_index).astype(jnp.float32)
        term = jnp.einsum("tab,trb->tra", slab, picked, precision=highest_precision)
        return running + term * live[:, None, None]

    near_total = lax.fori_loop(
        0, busiest, near_step, jnp.zeros((leaves_here, RHS, LEAF), jnp.float32)
    )
    coef_blocks = coef_ext.reshape(RHS, 3 * leaves_here, K)
    picked_coef = jnp.take(coef_blocks, leaf_source - window_start, axis=1)
    leaf_far = jnp.einsum(
        "tjkl,rtjl->tkr",
        leaf_coupling.reshape(leaves_here, FAR0, K, K),
        picked_coef,
        precision=highest_precision,
    )
    transfers = leaf_transfer.reshape(leaves_here, K, K)
    lifted = jnp.einsum("tkl,tlr->tkr", transfers, leaf_coef, precision=highest_precision)
    cluster_coef = lifted.reshape(clusters_here, leaves_here // clusters_here, K, RHS).sum(axis=1)
    cluster_rows = cluster_coef.reshape(clusters_here, K * RHS)
    couplings = cluster_coupling.reshape(clusters_here, FAR1, K, K)
    shard_rows = lax.all_gather(cluster_rows, "leaf", axis=0, tiled=True)
    onehot = (cluster_source[:, :, None] == jnp.arange(shard_rows.shape[0])[None, None, :]).astype(
        jnp.float32
    )
    selected = jnp.einsum("ujn,nm->ujm", onehot, shard_rows, precision=highest_precision)
    selected = selected.reshape(clusters_here, FAR1, K, RHS)
    cluster_far = jnp.einsum("ujkl,ujlr->ukr", couplings, selected, precision=highest_precision)
    upper = cluster_transfer.reshape(clusters_here, K, K)
    projected = jnp.einsum("ukl,ulr->ukr", upper, cluster_coef, precision=highest_precision)
    projected_sum = projected.sum(axis=0).reshape(1, K * RHS)
    group_sum = lax.psum(projected_sum, "leaf")
    all_groups = lax.all_gather(group_sum, "group", axis=0, tiled=True)
    group_field = jnp.einsum(
        "hkl,hlr->kr",
        group_coupling.reshape(ngroups, K, K),
        all_groups.reshape(ngroups, K, RHS),
        precision=highest_precision,
    )
    cluster_field = cluster_far + jnp.einsum(
        "ulk,lr->ukr", upper, group_field, precision=highest_precision
    )
    spread_cluster = jnp.repeat(cluster_field, leaves_here // clusters_here, axis=0)
    leaf_field = leaf_far + jnp.einsum(
        "tlk,tlr->tkr", transfers, spread_cluster, precision=highest_precision
    )
    total = near_total + jnp.einsum("tka,tkr->tra", bases, leaf_field, precision=highest_precision)
    return total.transpose(1, 0, 2).reshape(RHS, leaves_here * LEAF)


def solution(mesh):
    in_specs = (
        P(None, ("group", "leaf")),
        P(("group", "leaf"), None, None),
        P(("group", "leaf"), None),
        P(("group", "leaf")),
        P(("group", "leaf"), None),
        P(("group", "leaf"), None),
        P(("group", "leaf"), None, None),
        P(("group", "leaf"), None),
        P(("group", "leaf"), None),
        P(("group", "leaf"), None, None),
        P(("group", "leaf"), None),
        P("group", None, None),
    )
    out_specs = P(None, ("group", "leaf"))
    return jax.shard_map(
        per_device, mesh=mesh, in_specs=in_specs, out_specs=out_specs, check_vma=False
    )
```

profile of v0, /device:TPU:0, one launch (start us, length us, event | category | flops | bytes accessed | tf_op | source)
XLA Modules:
  0.0 376.4 jit_solution(737260132806493097)
XLA Ops:
  1.4 3.7 collective-permute-start
  12.2 3.7 collective-permute-start.2
  18.9 60.3 %all-gather = f32[64,4,512]{2,1,0:T(4,128)S(1)} all-gather(f32[1,4,512]{2,1,0:T(4,128)S(1)} %reshape.105), channel_id=1, replica_groups=mesh['group'=4,'leaf'=64] {'leaf'}, dimensions={0}, use_global_device_ids=true | all-gather | bytes 532480 | tf_op jit(solution)/shard_map/all_gather | solution.py:81
  83.3 126.7 %psum.7 = f32[1,512]{1,0:T(1,128)S(1)} all-reduce(f32[1,512]{1,0:T(1,128)S(1)} %reshape.82), channel_id=1, replica_groups=mesh['group'=4,'leaf'=64] {'leaf'}, use_global_device_ids=true, to_apply=%region_4.5 | all-reduce | flops 512 | bytes 4096 | tf_op jit(solution)/shard_map/psum | solution.py:91
  209.9 11.2 %all-gather.1 = f32[4,1,512]{2,1,0:T(1,128)S(1)} all-gather(f32[1,1,512]{2,1,0:T(1,128)S(1)} %bitcast.75), channel_id=1, replica_groups=mesh['group'=4,'leaf'=64] {'group'}, dimensions={0}, use_global_device_ids=true | all-gather | bytes 10240 | tf_op jit(solution)/shard_map/all_gather | solution.py:92
  222.9 3.8 %copy.82 = f32[64,8,1024]{0,2,1:T(8,128)} copy(f32[64,8,1024]{2,1,0:T(8,128)} %param.20) | data formatting | bytes 4194304 | tf_op args[6]
  226.7 9.1 %copy.83 = f32[64,8,32,32]{3,2,1,0:T(8,128)} copy(f32[64,8,32,32]{0,3,2,1:T(8,128)} %bitcast.67) | data formatting | bytes 4194304 | tf_op jit(solution)/shard_map/reshape | solution.py:72
  241.6 3.1 gather_fusion.1
  244.6 10.6 %fusion.10 = f32[64,16,32]{2,1,0:T(8,128)S(1)} fusion(f32[64,8,32,32]{3,2,1,0:T(8,128)} %copy.83, f32[64,8,16,32]{3,2,1,0:T(8,128)} %bitcast.68, pred[64,8]{1,0:T(8,128)(4,1)S(1)} %copy.76), kind=kOutput, calls=%fused_computation.19 | convolution fusion | flops 100925440 | bytes 3277312 | tf_op jit(solution)/shard_map/tjkl,rtjl->tkr/dot_general | solution.py:70
  258.7 2.1 copy.74
  261.6 111.1 %while.10 = (s32[]{:T(128)}, f32[64,16,64]{2,1,0:T(8,128)}, s32[]{:T(128)}, s32[64,8]{0,1:T(8,128)S(1)}, f32[192,16,64]{2,1,0:T(8,128)}, /*index=5*/f32[64,8,409...) while((s32[]{:T(128)}, f32[64,16,64]{2,1,0:T(8,128)}, s32[]{:T(128)}, ...), condition=%wide.region_2.0_spmd, body=%wide.region_1.2_spmd.sunk | while | flops 50529796 | bytes 8656923 | solution.py:65
  262.4 4.4 %constant_dynamic-slice_fusion.2 = f32[64,1,4096]{2,1,0:T(1,128)S(1)} fusion(f32[64,8,4096]{2,1,0:T(8,128)} %get-tuple-element.170, s32[]{:T(128)S(6)} %select_n.43), kind=kLoop, calls=%fused_computation.11.clone.1 | loop fusion | bytes 2097156 | tf_op jit(solution)/shard_map/while/body/jit(dynamic_index_in_dim)/dynamic_slice | solution.py:58
  268.4 2.0 gather_fusion
  270.4 5.3 %fusion.45 = f32[64,16,64]{2,1,0:T(8,128)} fusion(f32[64,16,64]{2,1,0:T(8,128)} %get-tuple-element.156, f32[64,64,64]{2,1,0:T(8,128)S(1)} %reshape.124, f32[64,16,64]{2,1,0:T(8,128)S(1)} %gather_fusion, f32[64]{0:T(128)S(1)} %compare_convert_fusion.2, pred[64]{0:T(512)(128)(4,1)S(1)} %get-tuple-element.144), kind=kOutput, calls=%fused_computation.3.clone.1 | convolution fusion | flops 50528256 | bytes 1835328 | tf_op jit(solution)/shard_map/while/body/tab,trb->tra/dot_general | solution.py:62
  276.2 4.4 %constant_dynamic-slice_fusion.2 = f32[64,1,4096]{2,1,0:T(1,128)S(1)} fusion(f32[64,8,4096]{2,1,0:T(8,128)} %get-tuple-element.170, s32[]{:T(128)S(6)} %select_n.43), kind=kLoop, calls=%fused_computation.11.clone.1 | loop fusion | bytes 2097156 | tf_op jit(solution)/shard_map/while/body/jit(dynamic_index_in_dim)/dynamic_slice | solution.py:58
  282.2 2.0 gather_fusion
  284.2 5.3 %fusion.45 = f32[64,16,64]{2,1,0:T(8,128)} fusion(f32[64,16,64]{2,1,0:T(8,128)} %get-tuple-element.156, f32[64,64,64]{2,1,0:T(8,128)S(1)} %reshape.124, f32[64,16,64]{2,1,0:T(8,128)S(1)} %gather_fusion, f32[64]{0:T(128)S(1)} %compare_convert_fusion.2, pred[64]{0:T(512)(128)(4,1)S(1)} %get-tuple-element.144), kind=kOutput, calls=%fused_computation.3.clone.1 | convolution fusion | flops 50528256 | bytes 1835328 | tf_op jit(solution)/shard_map/while/body/tab,trb->tra/dot_general | solution.py:62
  290.0 4.4 %constant_dynamic-slice_fusion.2 = f32[64,1,4096]{2,1,0:T(1,128)S(1)} fusion(f32[64,8,4096]{2,1,0:T(8,128)} %get-tuple-element.170, s32[]{:T(128)S(6)} %select_n.43), kind=kLoop, calls=%fused_computation.11.clone.1 | loop fusion | bytes 2097156 | tf_op jit(solution)/shard_map/while/body/jit(dynamic_index_in_dim)/dynamic_slice | solution.py:58
  298.0 5.3 %fusion.45 = f32[64,16,64]{2,1,0:T(8,128)} fusion(f32[64,16,64]{2,1,0:T(8,128)} %get-tuple-element.156, f32[64,64,64]{2,1,0:T(8,128)S(1)} %reshape.124, f32[64,16,64]{2,1,0:T(8,128)S(1)} %gather_fusion, f32[64]{0:T(128)S(1)} %compare_convert_fusion.2, pred[64]{0:T(512)(128)(4,1)S(1)} %get-tuple-element.144), kind=kOutput, calls=%fused_computation.3.clone.1 | convolution fusion | flops 50528256 | bytes 1835328 | tf_op jit(solution)/shard_map/while/body/tab,trb->tra/dot_general | solution.py:62
  303.8 4.4 %constant_dynamic-slice_fusion.2 = f32[64,1,4096]{2,1,0:T(1,128)S(1)} fusion(f32[64,8,4096]{2,1,0:T(8,128)} %get-tuple-element.170, s32[]{:T(128)S(6)} %select_n.43), kind=kLoop, calls=%fused_computation.11.clone.1 | loop fusion | bytes 2097156 | tf_op jit(solution)/shard_map/while/body/jit(dynamic_index_in_dim)/dynamic_slice | solution.py:58
  311.8 5.3 %fusion.45 = f32[64,16,64]{2,1,0:T(8,128)} fusion(f32[64,16,64]{2,1,0:T(8,128)} %get-tuple-element.156, f32[64,64,64]{2,1,0:T(8,128)S(1)} %reshape.124, f32[64,16,64]{2,1,0:T(8,128)S(1)} %gather_fusion, f32[64]{0:T(128)S(1)} %compare_convert_fusion.2, pred[64]{0:T(512)(128)(4,1)S(1)} %get-tuple-element.144), kind=kOutput, calls=%fused_computation.3.clone.1 | convolution fusion | flops 50528256 | bytes 1835328 | tf_op jit(solution)/shard_map/while/body/tab,trb->tra/dot_general | solution.py:62
  317.6 4.4 %constant_dynamic-slice_fusion.2 = f32[64,1,4096]{2,1,0:T(1,128)S(1)} fusion(f32[64,8,4096]{2,1,0:T(8,128)} %get-tuple-element.170, s32[]{:T(128)S(6)} %select_n.43), kind=kLoop, calls=%fused_computation.11.clone.1 | loop fusion | bytes 2097156 | tf_op jit(solution)/shard_map/while/body/jit(dynamic_index_in_dim)/dynamic_slice | solution.py:58
  325.5 5.3 %fusion.45 = f32[64,16,64]{2,1,0:T(8,128)} fusion(f32[64,16,64]{2,1,0:T(8,128)} %get-tuple-element.156, f32[64,64,64]{2,1,0:T(8,128)S(1)} %reshape.124, f32[64,16,64]{2,1,0:T(8,128)S(1)} %gather_fusion, f32[64]{0:T(128)S(1)} %compare_convert_fusion.2, pred[64]{0:T(512)(128)(4,1)S(1)} %get-tuple-element.144), kind=kOutput, calls=%fused_computation.3.clone.1 | convolution fusion | flops 50528256 | bytes 1835328 | tf_op jit(solution)/shard_map/while/body/tab,trb->tra/dot_general | solution.py:62
  331.4 4.4 %constant_dynamic-slice_fusion.2 = f32[64,1,4096]{2,1,0:T(1,128)S(1)} fusion(f32[64,8,4096]{2,1,0:T(8,128)} %get-tuple-element.170, s32[]{:T(128)S(6)} %select_n.43), kind=kLoop, calls=%fused_computation.11.clone.1 | loop fusion | bytes 2097156 | tf_op jit(solution)/shard_map/while/body/jit(dynamic_index_in_dim)/dynamic_slice | solution.py:58
  339.3 5.3 %fusion.45 = f32[64,16,64]{2,1,0:T(8,128)} fusion(f32[64,16,64]{2,1,0:T(8,128)} %get-tuple-element.156, f32[64,64,64]{2,1,0:T(8,128)S(1)} %reshape.124, f32[64,16,64]{2,1,0:T(8,128)S(1)} %gather_fusion, f32[64]{0:T(128)S(1)} %compare_convert_fusion.2, pred[64]{0:T(512)(128)(4,1)S(1)} %get-tuple-element.144), kind=kOutput, calls=%fused_computation.3.clone.1 | convolution fusion | flops 50528256 | bytes 1835328 | tf_op jit(solution)/shard_map/while/body/tab,trb->tra/dot_general | solution.py:62
  345.2 4.4 %constant_dynamic-slice_fusion.2 = f32[64,1,4096]{2,1,0:T(1,128)S(1)} fusion(f32[64,8,4096]{2,1,0:T(8,128)} %get-tuple-element.170, s32[]{:T(128)S(6)} %select_n.43), kind=kLoop, calls=%fused_computation.11.clone.1 | loop fusion | bytes 2097156 | tf_op jit(solution)/shard_map/while/body/jit(dynamic_index_in_dim)/dynamic_slice | solution.py:58
  351.1 2.0 gather_fusion
  353.1 5.3 %fusion.45 = f32[64,16,64]{2,1,0:T(8,128)} fusion(f32[64,16,64]{2,1,0:T(8,128)} %get-tuple-element.156, f32[64,64,64]{2,1,0:T(8,128)S(1)} %reshape.124, f32[64,16,64]{2,1,0:T(8,128)S(1)} %gather_fusion, f32[64]{0:T(128)S(1)} %compare_convert_fusion.2, pred[64]{0:T(512)(128)(4,1)S(1)} %get-tuple-element.144), kind=kOutput, calls=%fused_computation.3.clone.1 | convolution fusion | flops 50528256 | bytes 1835328 | tf_op jit(solution)/shard_map/while/body/tab,trb->tra/dot_general | solution.py:62
  359.0 4.4 %constant_dynamic-slice_fusion.2 = f32[64,1,4096]{2,1,0:T(1,128)S(1)} fusion(f32[64,8,4096]{2,1,0:T(8,128)} %get-tuple-element.170, s32[]{:T(128)S(6)} %select_n.43), kind=kLoop, calls=%fused_computation.11.clone.1 | loop fusion | bytes 2097156 | tf_op jit(solution)/shard_map/while/body/jit(dynamic_index_in_dim)/dynamic_slice | solution.py:58
  364.9 2.0 gather_fusion
  366.9 5.3 %fusion.45 = f32[64,16,64]{2,1,0:T(8,128)} fusion(f32[64,16,64]{2,1,0:T(8,128)} %get-tuple-element.156, f32[64,64,64]{2,1,0:T(8,128)S(1)} %reshape.124, f32[64,16,64]{2,1,0:T(8,128)S(1)} %gather_fusion, f32[64]{0:T(128)S(1)} %compare_convert_fusion.2, pred[64]{0:T(512)(128)(4,1)S(1)} %get-tuple-element.144), kind=kOutput, calls=%fused_computation.3.clone.1 | convolution fusion | flops 50528256 | bytes 1835328 | tf_op jit(solution)/shard_map/while/body/tab,trb->tra/dot_general | solution.py:62
  372.7 2.6 fusion.13
  (111 shorter events, 47.9 us)
Async XLA Ops:
  0.0 15.8 %copy-start.2 = (f32[64,1024]{1,0:T(8,128)S(1)}, f32[64,1024]{1,0:T(8,128)}, u32[]{:S(2)}) copy-start(f32[64,1024]{1,0:T(8,128)} %param.21) | copy-start | bytes 786436
  0.0 257.1 %collective-permute-start.1 = (f32[16,4096]{1,0:T(8,128)}, f32[16,4096]{1,0:T(8,128)S(1)}, u32[]{:S(2)}, u32[]{:S(2)}) collective-permute-start(f32[16,4096]{1,0:T(8,128)} %param.14), channel_id=1, source_target_pairs={{1,0},{2,1},{3,2},{4,3},{5,4},{6,5},{7,6},{8,7},{9,8},{10,9},{11,1... | collective-permute-start | bytes 786440 | tf_op jit(solution)/shard_map/ppermute | solution.py:22
  1.4 255.7 %collective-permute-start = (f32[16,4096]{1,0:T(8,128)}, f32[16,4096]{1,0:T(8,128)}, u32[]{:S(2)}, u32[]{:S(2)}) collective-permute-start(f32[16,4096]{1,0:T(8,128)} %param.14), channel_id=1, source_target_pairs={{0,1},{1,2},{2,3},{3,4},{4,5},{5,6},{6,7},{7,8},{8,9},{9,10},{10,1... | collective-permute-start | bytes 786440 | tf_op jit(solution)/shard_map/ppermute | solution.py:21
  7.8 71.4 %copy-start = (f32[64,32,64]{2,1,0:T(8,128)}, f32[64,32,64]{2,1,0:T(8,128)S(1)}, u32[]{:S(2)}) copy-start(f32[64,32,64]{2,1,0:T(8,128)S(1)} %reshape.72) | copy-start | bytes 1572868
  9.7 70.4 %copy-start.7 = (s32[4,8]{1,0:T(4,128)S(1)}, s32[4,8]{1,0:T(4,128)}, u32[]{:S(2)}) copy-start(s32[4,8]{1,0:T(4,128)} %param.22) | copy-start | bytes 388
  9.9 72.9 %copy-start.3 = (f32[4,1024]{1,0:T(4,128)S(1)}, f32[4,1024]{1,0:T(4,128)}, u32[]{:S(2)}) copy-start(f32[4,1024]{1,0:T(4,128)} %param.24) | copy-start | bytes 49156
  9.9 211.4 %copy-start.4 = (f32[1,4,1024]{2,1,0:T(4,128)S(1)}, f32[1,4,1024]{2,1,0:T(4,128)}, u32[]{:S(2)}) copy-start(f32[1,4,1024]{2,1,0:T(4,128)} %param.25) | copy-start | bytes 49156
  10.0 211.4 %copy-start.5 = (s32[64,8]{0,1:T(8,128)S(1)}, s32[64,8]{0,1:T(8,128)}, u32[]{:S(2)}) copy-start(s32[64,8]{0,1:T(8,128)} %param.19) | copy-start | bytes 6148
  10.9 225.9 %collective-permute-start.3 = (f32[16,2048]{1,0:T(8,128)}, f32[16,2048]{1,0:T(8,128)}, u32[]{:S(2)}, u32[]{:S(2)}) collective-permute-start(f32[16,2048]{1,0:T(8,128)} %reshape.74), channel_id=1, source_target_pairs={{1,0},{2,1},{3,2},{4,3},{5,4},{6,5},{7,6},{8,7},{9,8},{10,9},{11,1... | collective-permute-start | bytes 393224 | tf_op jit(solution)/shard_map/ppermute | solution.py:22
  12.2 226.9 %collective-permute-start.2 = (f32[16,2048]{1,0:T(8,128)}, f32[16,2048]{1,0:T(8,128)}, u32[]{:S(2)}, u32[]{:S(2)}) collective-permute-start(f32[16,2048]{1,0:T(8,128)} %reshape.74), channel_id=1, source_target_pairs={{0,1},{1,2},{2,3},{3,4},{4,5},{5,6},{6,7},{7,8},{8,9},{9,10},{10,1... | collective-permute-start | bytes 393224 | tf_op jit(solution)/shard_map/ppermute | solution.py:21
  16.0 206.8 %copy-start.6 = (s32[64,8]{0,1:T(8,128)S(1)}, s32[64,8]{0,1:T(8,128)}, u32[]{:S(2)}) copy-start(s32[64,8]{0,1:T(8,128)} %param.16) | copy-start | bytes 6148
  226.7 9.4 %copy-start.8 = (s32[64]{0:T(128)S(1)}, s32[64]{0:T(128)}, u32[]{:S(2)}) copy-start(s32[64]{0:T(128)} %param.17) | copy-start | bytes 772
  244.6 12.5 %copy-start.1 = (f32[16,4096]{1,0:T(8,128)S(1)}, f32[16,4096]{1,0:T(8,128)}, u32[]{:S(2)}) copy-start(f32[16,4096]{1,0:T(8,128)} %param.14) | copy-start | bytes 786436
where the time goes:
time: 378 us; the launch traced here: 376 us
  blocking collectives  198 us (52%)
  local copies, waits for them, and re-layouts  95.3 us (25%)
  matrix products  63.6 us (17%)
  starting transfers between devices  10.1 us (3%)
  loops' own time  5.86 us (2%)
    psum x1, blocking collectives, per_device(): group_sum = lax.psum(projected_sum, 'leaf')  127 us
    all_gather x1, blocking collectives, per_device(): shard_rows = lax.all_gather(cluster_rows, 'leaf', axis=0, tiled=True)  60.3 us
    dot_general x8, matrix products, near_step(): term = jnp.einsum('tab,trb->tra', slab, picked, precision=highest_precision)  42 us
    dynamic_slice x16, local copies, waits for them, and re-layouts, near_step(): lax.dynamic_index_in_dim(near_blocks, slot_index, axis=1, keepdims=False)  40.3 us
    gather x8, local copies, waits for them, and re-layouts, near_step(): picked = jnp.take(point_blocks, near_local[:, slot_index], axis=0)  16 us
    all_gather x1, blocking collectives, per_device(): all_groups = lax.all_gather(group_sum, 'group', axis=0, tiled=True)  11.2 us
    dot_general x1, matrix products, per_device(): jnp.einsum('tjkl,rtjl->tkr', leaf_coupling.reshape(leaves_here, FAR0, K,...  10.6 us
    reshape x1, local copies, waits for them, and re-layouts, per_device(): leaf_coupling.reshape(leaves_here, FAR0, K, K)  9.12 us
  transfers between devices with their start and end apart: 4, of which 0 were waited for; matrix products, arithmetic and copies ran while one was open for 13% of the time, Pallas kernels for 0%

commit v1 on v0

--- a/solution.py
+++ b/solution.py
@@ -78,7 +78,9 @@
     cluster_coef = lifted.reshape(clusters_here, leaves_here // clusters_here, K, RHS).sum(axis=1)
     cluster_rows = cluster_coef.reshape(clusters_here, K * RHS)
     couplings = cluster_coupling.reshape(clusters_here, FAR1, K, K)
-    shard_rows = lax.all_gather(cluster_rows, "leaf", axis=0, tiled=True)
+    shard_rows = jnp.concatenate(
+        lax.all_to_all(jnp.stack([cluster_rows] * lax.axis_size("leaf")), "leaf", 0, 0), axis=0
+    )
     onehot = (cluster_source[:, :, None] == jnp.arange(shard_rows.shape[0])[None, None, :]).astype(
         jnp.float32
     )

time: 378 us -> 344 us (0.910)
  blocking collectives: 198 us -> 142 us
  starting transfers between devices: 10.1 us -> 28.3 us
    all_gather x1 -> x0, blocking collectives: 60.3 us -> none  [per_device(): shard_rows = lax.all_gather(cluster_rows, 'leaf', axis=0, tiled=True)]
    all_to_all x0 -> x1, starting transfers between devices: none -> 18.1 us  [per_device(): lax.all_to_all(jnp.stack([cluster_rows] * lax.axis_size('leaf')), 'leaf',...]
    psum x1, blocking collectives: 127 us -> 131 us  [per_device(): group_sum = lax.psum(projected_sum, 'leaf')]
  transfers between devices with their start and end apart: 4 -> 5, of which waited for: 0 -> 0; matrix products, arithmetic and copies ran while one was open for 13% -> 45% of each run, Pallas kernels for 0% -> 0%
where the time goes in v1:
time: 344 us; the launch traced here: 341 us
  blocking collectives  142 us (41%)
  local copies, waits for them, and re-layouts  98.4 us (29%)
  matrix products  63.5 us (18%)
  starting transfers between devices  28.3 us (8%)
  loops' own time  5.99 us (2%)
    psum x1, blocking collectives, per_device(): group_sum = lax.psum(projected_sum, 'leaf')  131 us
    dot_general x8, matrix products, near_step(): term = jnp.einsum('tab,trb->tra', slab, picked, precision=highest_precision)  42.1 us
    dynamic_slice x16, local copies, waits for them, and re-layouts, near_step(): lax.dynamic_index_in_dim(near_blocks, slot_index, axis=1, keepdims=False)  40.3 us
    all_to_all x1, starting transfers between devices, per_device(): lax.all_to_all(jnp.stack([cluster_rows] * lax.axis_size('leaf')), 'leaf',...  18.1 us
    gather x8, local copies, waits for them, and re-layouts, near_step(): picked = jnp.take(point_blocks, near_local[:, slot_index], axis=0)  16 us
    dot_general x1, matrix products, per_device(): jnp.einsum('tjkl,rtjl->tkr', leaf_coupling.reshape(leaves_here, FAR0, K,...  11.4 us
    all_gather x1, blocking collectives, per_device(): all_groups = lax.all_gather(group_sum, 'group', axis=0, tiled=True)  11.2 us
    reshape x1, local copies, waits for them, and re-layouts, per_device(): leaf_coupling.reshape(leaves_here, FAR0, K, K)  9.15 us
  transfers between devices with their start and end apart: 5, of which 0 were waited for; matrix products, arithmetic and copies ran while one was open for 45% of the time, Pallas kernels for 0%

profile of v1, /device:TPU:0, one launch (start us, length us, event | category | flops | bytes accessed | tf_op | source)
XLA Modules:
  0.0 340.6 jit_solution(17616240980550156632)
XLA Ops:
  1.4 3.8 %collective-permute-start = (f32[16,4096]{1,0:T(8,128)}, f32[16,4096]{1,0:T(8,128)}, u32[]{:S(2)}, u32[]{:S(2)}) collective-permute-start(f32[16,4096]{1,0:T(8,128)} %param.14), channel_id=1, source_target_pairs={{0,1},{1,2},{2,3},{3,4},{4,5},{5,6},{6,7},{7,8},{8,9},{9,10},{10,1... | collective-permute-start | bytes 786440 | tf_op jit(solution)/shard_map/ppermute | solution.py:21
  12.2 3.7 %collective-permute-start.2 = (f32[16,2048]{1,0:T(8,128)}, f32[16,2048]{1,0:T(8,128)}, u32[]{:S(2)}, u32[]{:S(2)}) collective-permute-start(f32[16,2048]{1,0:T(8,128)} %reshape.75), channel_id=1, source_target_pairs={{0,1},{1,2},{2,3},{3,4},{4,5},{5,6},{6,7},{7,8},{8,9},{9,10},{10,1... | collective-permute-start | bytes 393224 | tf_op jit(solution)/shard_map/ppermute | solution.py:21
  19.9 18.1 %all-to-all-start = ((f32[64,4,512]{2,1,0:T(4,128)}), f32[64,4,512]{2,1,0:T(4,128)}, u32[]{:S(2)}, u32[]{:S(2)}) async-start(f32[64,4,512]{2,1,0:T(4,128)} %stack.3), calls=%async_computation | async-start | bytes 1048576 | tf_op jit(solution)/shard_map/all_to_all | solution.py:82
  38.4 130.9 %psum.7 = f32[1,512]{1,0:T(1,128)S(1)} all-reduce(f32[1,512]{1,0:T(1,128)S(1)} %reshape.82), channel_id=1, replica_groups=mesh['group'=4,'leaf'=64] {'leaf'}, use_global_device_ids=true, to_apply=%region_4.5 | all-reduce | flops 512 | bytes 4096 | tf_op jit(solution)/shard_map/psum | solution.py:93
  169.3 11.2 %all-gather = f32[4,1,512]{2,1,0:T(1,128)S(1)} all-gather(f32[1,1,512]{2,1,0:T(1,128)S(1)} %bitcast.85), channel_id=1, replica_groups=mesh['group'=4,'leaf'=64] {'group'}, dimensions={0}, use_global_device_ids=true | all-gather | bytes 10240 | tf_op jit(solution)/shard_map/all_gather | solution.py:94
  181.0 3.8 %copy.105 = f32[64,8,1024]{0,2,1:T(8,128)} copy(f32[64,8,1024]{2,1,0:T(8,128)} %param.20) | data formatting | bytes 4194304 | tf_op args[6]
  184.9 9.2 %copy.106 = f32[64,8,32,32]{3,2,1,0:T(8,128)} copy(f32[64,8,32,32]{0,3,2,1:T(8,128)} %bitcast.75) | data formatting | bytes 4194304 | tf_op jit(solution)/shard_map/reshape | solution.py:72
  198.9 3.1 gather_fusion.1
  202.0 11.4 %fusion.10 = f32[64,16,32]{2,1,0:T(8,128)} fusion(f32[64,8,32,32]{3,2,1,0:T(8,128)} %copy.106, f32[64,8,16,32]{3,2,1,0:T(8,128)} %bitcast.76, pred[64,8]{1,0:T(8,128)(4,1)S(1)} %copy.99), kind=kOutput, calls=%fused_computation.19 | convolution fusion | flops 100925440 | bytes 3277312 | tf_op jit(solution)/shard_map/tjkl,rtjl->tkr/dot_general | solution.py:70
  215.0 2.1 copy.97
  218.0 111.3 %while.10 = (s32[]{:T(128)}, f32[64,16,64]{2,1,0:T(8,128)}, s32[]{:T(128)}, s32[64,8]{0,1:T(8,128)S(1)}, f32[192,16,64]{2,1,0:T(8,128)}, /*index=5*/f32[64,8,409...) while((s32[]{:T(128)}, f32[64,16,64]{2,1,0:T(8,128)}, s32[]{:T(128)}, ...), condition=%wide.region_2.0_spmd, body=%wide.region_1.2_spmd.sunk | while | flops 50529796 | bytes 8656923 | solution.py:65
  218.8 4.4 %constant_dynamic-slice_fusion.2 = f32[64,1,4096]{2,1,0:T(1,128)S(1)} fusion(f32[64,8,4096]{2,1,0:T(8,128)} %get-tuple-element.177, s32[]{:T(128)S(6)} %select_n.43), kind=kLoop, calls=%fused_computation.11.clone.1 | loop fusion | bytes 2097156 | tf_op jit(solution)/shard_map/while/body/jit(dynamic_index_in_dim)/dynamic_slice | solution.py:58
  224.7 2.0 gather_fusion
  226.8 5.3 %fusion.48 = f32[64,16,64]{2,1,0:T(8,128)} fusion(f32[64,16,64]{2,1,0:T(8,128)} %get-tuple-element.163, f32[64,64,64]{2,1,0:T(8,128)S(1)} %reshape.121, f32[64,16,64]{2,1,0:T(8,128)S(1)} %gather_fusion, f32[64]{0:T(128)S(1)} %compare_convert_fusion.2, pred[64]{0:T(512)(128)(4,1)S(1)} %get-tuple-element.151), kind=kOutput, calls=%fused_computation.3.clone.1 | convolution fusion | flops 50528256 | bytes 1835328 | tf_op jit(solution)/shard_map/while/body/tab,trb->tra/dot_general | solution.py:62
  232.6 4.4 %constant_dynamic-slice_fusion.2 = f32[64,1,4096]{2,1,0:T(1,128)S(1)} fusion(f32[64,8,4096]{2,1,0:T(8,128)} %get-tuple-element.177, s32[]{:T(128)S(6)} %select_n.43), kind=kLoop, calls=%fused_computation.11.clone.1 | loop fusion | bytes 2097156 | tf_op jit(solution)/shard_map/while/body/jit(dynamic_index_in_dim)/dynamic_slice | solution.py:58
  238.6 2.0 gather_fusion
  240.6 5.3 %fusion.48 = f32[64,16,64]{2,1,0:T(8,128)} fusion(f32[64,16,64]{2,1,0:T(8,128)} %get-tuple-element.163, f32[64,64,64]{2,1,0:T(8,128)S(1)} %reshape.121, f32[64,16,64]{2,1,0:T(8,128)S(1)} %gather_fusion, f32[64]{0:T(128)S(1)} %compare_convert_fusion.2, pred[64]{0:T(512)(128)(4,1)S(1)} %get-tuple-element.151), kind=kOutput, calls=%fused_computation.3.clone.1 | convolution fusion | flops 50528256 | bytes 1835328 | tf_op jit(solution)/shard_map/while/body/tab,trb->tra/dot_general | solution.py:62
  246.4 4.4 %constant_dynamic-slice_fusion.2 = f32[64,1,4096]{2,1,0:T(1,128)S(1)} fusion(f32[64,8,4096]{2,1,0:T(8,128)} %get-tuple-element.177, s32[]{:T(128)S(6)} %select_n.43), kind=kLoop, calls=%fused_computation.11.clone.1 | loop fusion | bytes 2097156 | tf_op jit(solution)/shard_map/while/body/jit(dynamic_index_in_dim)/dynamic_slice | solution.py:58
  252.4 2.0 gather_fusion
  254.4 5.3 %fusion.48 = f32[64,16,64]{2,1,0:T(8,128)} fusion(f32[64,16,64]{2,1,0:T(8,128)} %get-tuple-element.163, f32[64,64,64]{2,1,0:T(8,128)S(1)} %reshape.121, f32[64,16,64]{2,1,0:T(8,128)S(1)} %gather_fusion, f32[64]{0:T(128)S(1)} %compare_convert_fusion.2, pred[64]{0:T(512)(128)(4,1)S(1)} %get-tuple-element.151), kind=kOutput, calls=%fused_computation.3.clone.1 | convolution fusion | flops 50528256 | bytes 1835328 | tf_op jit(solution)/shard_map/while/body/tab,trb->tra/dot_general | solution.py:62
  260.3 4.4 %constant_dynamic-slice_fusion.2 = f32[64,1,4096]{2,1,0:T(1,128)S(1)} fusion(f32[64,8,4096]{2,1,0:T(8,128)} %get-tuple-element.177, s32[]{:T(128)S(6)} %select_n.43), kind=kLoop, calls=%fused_computation.11.clone.1 | loop fusion | bytes 2097156 | tf_op jit(solution)/shard_map/while/body/jit(dynamic_index_in_dim)/dynamic_slice | solution.py:58
  268.2 5.3 %fusion.48 = f32[64,16,64]{2,1,0:T(8,128)} fusion(f32[64,16,64]{2,1,0:T(8,128)} %get-tuple-element.163, f32[64,64,64]{2,1,0:T(8,128)S(1)} %reshape.121, f32[64,16,64]{2,1,0:T(8,128)S(1)} %gather_fusion, f32[64]{0:T(128)S(1)} %compare_convert_fusion.2, pred[64]{0:T(512)(128)(4,1)S(1)} %get-tuple-element.151), kind=kOutput, calls=%fused_computation.3.clone.1 | convolution fusion | flops 50528256 | bytes 1835328 | tf_op jit(solution)/shard_map/while/body/tab,trb->tra/dot_general | solution.py:62
  274.1 4.4 %constant_dynamic-slice_fusion.2 = f32[64,1,4096]{2,1,0:T(1,128)S(1)} fusion(f32[64,8,4096]{2,1,0:T(8,128)} %get-tuple-element.177, s32[]{:T(128)S(6)} %select_n.43), kind=kLoop, calls=%fused_computation.11.clone.1 | loop fusion | bytes 2097156 | tf_op jit(solution)/shard_map/while/body/jit(dynamic_index_in_dim)/dynamic_slice | solution.py:58
  282.0 5.3 %fusion.48 = f32[64,16,64]{2,1,0:T(8,128)} fusion(f32[64,16,64]{2,1,0:T(8,128)} %get-tuple-element.163, f32[64,64,64]{2,1,0:T(8,128)S(1)} %reshape.121, f32[64,16,64]{2,1,0:T(8,128)S(1)} %gather_fusion, f32[64]{0:T(128)S(1)} %compare_convert_fusion.2, pred[64]{0:T(512)(128)(4,1)S(1)} %get-tuple-element.151), kind=kOutput, calls=%fused_computation.3.clone.1 | convolution fusion | flops 50528256 | bytes 1835328 | tf_op jit(solution)/shard_map/while/body/tab,trb->tra/dot_general | solution.py:62
  287.9 4.4 %constant_dynamic-slice_fusion.2 = f32[64,1,4096]{2,1,0:T(1,128)S(1)} fusion(f32[64,8,4096]{2,1,0:T(8,128)} %get-tuple-element.177, s32[]{:T(128)S(6)} %select_n.43), kind=kLoop, calls=%fused_computation.11.clone.1 | loop fusion | bytes 2097156 | tf_op jit(solution)/shard_map/while/body/jit(dynamic_index_in_dim)/dynamic_slice | solution.py:58
  295.8 5.3 %fusion.48 = f32[64,16,64]{2,1,0:T(8,128)} fusion(f32[64,16,64]{2,1,0:T(8,128)} %get-tuple-element.163, f32[64,64,64]{2,1,0:T(8,128)S(1)} %reshape.121, f32[64,16,64]{2,1,0:T(8,128)S(1)} %gather_fusion, f32[64]{0:T(128)S(1)} %compare_convert_fusion.2, pred[64]{0:T(512)(128)(4,1)S(1)} %get-tuple-element.151), kind=kOutput, calls=%fused_computation.3.clone.1 | convolution fusion | flops 50528256 | bytes 1835328 | tf_op jit(solution)/shard_map/while/body/tab,trb->tra/dot_general | solution.py:62
  301.7 4.4 %constant_dynamic-slice_fusion.2 = f32[64,1,4096]{2,1,0:T(1,128)S(1)} fusion(f32[64,8,4096]{2,1,0:T(8,128)} %get-tuple-element.177, s32[]{:T(128)S(6)} %select_n.43), kind=kLoop, calls=%fused_computation.11.clone.1 | loop fusion | bytes 2097156 | tf_op jit(solution)/shard_map/while/body/jit(dynamic_index_in_dim)/dynamic_slice | solution.py:58
  309.7 5.3 %fusion.48 = f32[64,16,64]{2,1,0:T(8,128)} fusion(f32[64,16,64]{2,1,0:T(8,128)} %get-tuple-element.163, f32[64,64,64]{2,1,0:T(8,128)S(1)} %reshape.121, f32[64,16,64]{2,1,0:T(8,128)S(1)} %gather_fusion, f32[64]{0:T(128)S(1)} %compare_convert_fusion.2, pred[64]{0:T(512)(128)(4,1)S(1)} %get-tuple-element.151), kind=kOutput, calls=%fused_computation.3.clone.1 | convolution fusion | flops 50528256 | bytes 1835328 | tf_op jit(solution)/shard_map/while/body/tab,trb->tra/dot_general | solution.py:62
  315.5 4.4 %constant_dynamic-slice_fusion.2 = f32[64,1,4096]{2,1,0:T(1,128)S(1)} fusion(f32[64,8,4096]{2,1,0:T(8,128)} %get-tuple-element.177, s32[]{:T(128)S(6)} %select_n.43), kind=kLoop, calls=%fused_computation.11.clone.1 | loop fusion | bytes 2097156 | tf_op jit(solution)/shard_map/while/body/jit(dynamic_index_in_dim)/dynamic_slice | solution.py:58
  323.5 5.3 %fusion.48 = f32[64,16,64]{2,1,0:T(8,128)} fusion(f32[64,16,64]{2,1,0:T(8,128)} %get-tuple-element.163, f32[64,64,64]{2,1,0:T(8,128)S(1)} %reshape.121, f32[64,16,64]{2,1,0:T(8,128)S(1)} %gather_fusion, f32[64]{0:T(128)S(1)} %compare_convert_fusion.2, pred[64]{0:T(512)(128)(4,1)S(1)} %get-tuple-element.151), kind=kOutput, calls=%fused_computation.3.clone.1 | convolution fusion | flops 50528256 | bytes 1835328 | tf_op jit(solution)/shard_map/while/body/tab,trb->tra/dot_general | solution.py:62
  329.4 2.2 reshape.79
  331.6 2.0 copy.110
  (125 shorter events, 49.1 us)
Async XLA Ops:
  0.0 15.9 %copy-start.7 = (f32[64,1024]{1,0:T(8,128)S(1)}, f32[64,1024]{1,0:T(8,128)}, u32[]{:S(2)}) copy-start(f32[64,1024]{1,0:T(8,128)} %param.21) | copy-start | bytes 786436
  0.0 213.4 %collective-permute-start.1 = (f32[16,4096]{1,0:T(8,128)}, f32[16,4096]{1,0:T(8,128)S(1)}, u32[]{:S(2)}, u32[]{:S(2)}) collective-permute-start(f32[16,4096]{1,0:T(8,128)} %param.14), channel_id=1, source_target_pairs={{1,0},{2,1},{3,2},{4,3},{5,4},{6,5},{7,6},{8,7},{9,8},{10,9},{11,1... | collective-permute-start | bytes 786440 | tf_op jit(solution)/shard_map/ppermute | solution.py:22
  1.4 212.0 %collective-permute-start = (f32[16,4096]{1,0:T(8,128)}, f32[16,4096]{1,0:T(8,128)}, u32[]{:S(2)}, u32[]{:S(2)}) collective-permute-start(f32[16,4096]{1,0:T(8,128)} %param.14), channel_id=1, source_target_pairs={{0,1},{1,2},{2,3},{3,4},{4,5},{5,6},{6,7},{7,8},{8,9},{9,10},{10,1... | collective-permute-start | bytes 786440 | tf_op jit(solution)/shard_map/ppermute | solution.py:21
  7.8 12.1 %copy-start.1 = (f32[64,32,64]{2,1,0:T(8,128)}, f32[64,32,64]{2,1,0:T(8,128)S(1)}, u32[]{:S(2)}) copy-start(f32[64,32,64]{2,1,0:T(8,128)S(1)} %reshape.73) | copy-start | bytes 1572868
  9.8 28.2 %copy-start.9 = (f32[4,1024]{1,0:T(4,128)S(1)}, f32[4,1024]{1,0:T(4,128)}, u32[]{:S(2)}) copy-start(f32[4,1024]{1,0:T(4,128)} %param.24) | copy-start | bytes 49156
  9.8 170.9 %copy-start.10 = (f32[1,4,1024]{2,1,0:T(4,128)S(1)}, f32[1,4,1024]{2,1,0:T(4,128)}, u32[]{:S(2)}) copy-start(f32[1,4,1024]{2,1,0:T(4,128)} %param.25) | copy-start | bytes 49156
  9.8 171.0 %copy-start.11 = (s32[64,8]{0,1:T(8,128)S(1)}, s32[64,8]{0,1:T(8,128)}, u32[]{:S(2)}) copy-start(s32[64,8]{0,1:T(8,128)} %param.19) | copy-start | bytes 6148
  9.8 171.2 %copy-start.12 = (s32[64,8]{0,1:T(8,128)S(1)}, s32[64,8]{0,1:T(8,128)}, u32[]{:S(2)}) copy-start(s32[64,8]{0,1:T(8,128)} %param.16) | copy-start | bytes 6148
  10.9 185.1 %collective-permute-start.3 = (f32[16,2048]{1,0:T(8,128)}, f32[16,2048]{1,0:T(8,128)}, u32[]{:S(2)}, u32[]{:S(2)}) collective-permute-start(f32[16,2048]{1,0:T(8,128)} %reshape.75), channel_id=1, source_target_pairs={{1,0},{2,1},{3,2},{4,3},{5,4},{6,5},{7,6},{8,7},{9,8},{10,9},{11,1... | collective-permute-start | bytes 393224 | tf_op jit(solution)/shard_map/ppermute | solution.py:22
  12.2 185.2 %collective-permute-start.2 = (f32[16,2048]{1,0:T(8,128)}, f32[16,2048]{1,0:T(8,128)}, u32[]{:S(2)}, u32[]{:S(2)}) collective-permute-start(f32[16,2048]{1,0:T(8,128)} %reshape.75), channel_id=1, source_target_pairs={{0,1},{1,2},{2,3},{3,4},{4,5},{5,6},{6,7},{7,8},{8,9},{9,10},{10,1... | collective-permute-start | bytes 393224 | tf_op jit(solution)/shard_map/ppermute | solution.py:21
  17.0 167.9 %copy-start.3 = (f32[64,32,32]{2,1,0:T(8,128)}, f32[64,32,32]{2,1,0:T(8,128)S(1)}, u32[]{:S(2)}) copy-start(f32[64,32,32]{2,1,0:T(8,128)S(1)} %copy.108) | copy-start | bytes 786436
  19.9 309.5 %all-to-all-start = ((f32[64,4,512]{2,1,0:T(4,128)}), f32[64,4,512]{2,1,0:T(4,128)}, u32[]{:S(2)}, u32[]{:S(2)}) async-start(f32[64,4,512]{2,1,0:T(4,128)} %stack.3), calls=%async_computation | async-start | bytes 1048576 | tf_op jit(solution)/shard_map/all_to_all | solution.py:82
  184.9 9.4 %copy-start.8 = (f32[4,8,1024]{2,1,0:T(8,128)S(1)}, f32[4,8,1024]{2,1,0:T(8,128)}, u32[]{:S(2)}) copy-start(f32[4,8,1024]{2,1,0:T(8,128)} %param.23) | copy-start | bytes 393220
  184.9 10.4 %copy-start.14 = (s32[64]{0:T(128)S(1)}, s32[64]{0:T(128)}, u32[]{:S(2)}) copy-start(s32[64]{0:T(128)} %param.17) | copy-start | bytes 772
  202.0 11.5 %copy-start.6 = (f32[16,4096]{1,0:T(8,128)S(1)}, f32[16,4096]{1,0:T(8,128)}, u32[]{:S(2)}) copy-start(f32[16,4096]{1,0:T(8,128)} %param.14) | copy-start | bytes 786436
  218.0 115.6 %copy-start.13 = (s32[4,8]{1,0:T(4,128)S(1)}, s32[4,8]{1,0:T(4,128)}, u32[]{:S(2)}) copy-start(s32[4,8]{1,0:T(4,128)} %param.22) | copy-start | bytes 388
  329.3 8.1 %copy-start.4 = (f32[64,32,32]{2,1,0:T(8,128)S(1)}, f32[64,32,32]{2,1,0:T(8,128)}, u32[]{:S(2)}) copy-start(f32[64,32,32]{2,1,0:T(8,128)} %copy-done.3) | copy-start | bytes 786436
  329.3 8.1 %copy-start.5 = (f32[64,16,32]{2,1,0:T(8,128)S(1)}, f32[64,16,32]{2,1,0:T(8,128)}, u32[]{:S(2)}) copy-start(f32[64,16,32]{2,1,0:T(8,128)} %fusion.10) | copy-start | bytes 393220
  329.4 9.1 %copy-start = (f32[64,16,64]{2,1,0:T(8,128)S(1)}, f32[64,16,64]{2,1,0:T(8,128)}, u32[]{:S(2)}) copy-start(f32[64,16,64]{2,1,0:T(8,128)} %get-tuple-element.43) | copy-start | bytes 786436
  329.4 9.1 %copy-start.2 = (f32[64,32,64]{2,1,0:T(8,128)S(1)}, f32[64,32,64]{2,1,0:T(8,128)}, u32[]{:S(2)}) copy-start(f32[64,32,64]{2,1,0:T(8,128)} %copy-done.1) | copy-start | bytes 1572868
